TPU v7x, 512 devices: a whole 4x8x8 slice. The times are simulated.
512 devices in a mesh: gx: 16 (over y, z_hi), gy: 32 (over x, z_lo, core).
Axes of the slice: x: 4, y: 8, z: 8 (z_hi: 2, z_lo: 4; z = z_hi * 4 + z_lo), core: 2. Of those that a mesh axis runs over, the one named last changes fastest.
Arguments:
- e_field: float32 [3, 8, 2048, 2048], P(None, None, 'gy', 'gx'), may hold values from -7 to 7
- h_field: float32 [3, 8, 2048, 2048], P(None, None, 'gy', 'gx'), may hold values from -7 to 7
- material: int32 [8, 2048, 2048], P(None, 'gy', 'gx'), may hold values from 0 to 7
- permittivity: float32 [8], replicated, may hold values from 1 to 12
- conductivity: float32 [8], replicated, may hold values from 0.01 to 2
- wire_layers: int32 [8], replicated, may hold values from 0 to 1, as said below
Outputs:
- e_next: float32 [3, 8, 2048, 2048], P(None, None, 'gy', 'gx')
- h_next: float32 [3, 8, 2048, 2048], P(None, None, 'gy', 'gx')
Inputs may be any that keep to these rules, and one draw needn't show every extreme that they name: `wire_layers`: exactly 4 entries are 1.
All inputs are finite; a program needn't handle non-finite values.
Results may differ from a plain program's by a relative error of at most 0.0004.
The roundings to bfloat16 on the way count: a program that leaves them out, or rounds other values in their place, can miss the bound.
Values may be sent and summed in bfloat16 or wider, within the bound.
A program may use at most 128 MiB of HBM per device.

v0:
```python
import math

import jax
import jax.numpy as jnp
from jax import lax
from jax.sharding import PartitionSpec as P

TIME_STEP = 0.9


def shifted(value, axis, steps):
    count = lax.axis_size(axis)
    pairs = [(source, (source + steps) % count) for source in range(count)]
    return lax.ppermute(value, axis, pairs)


def passed_along(shard, axis, by):
    devices = lax.axis_size(axis)
    pairs = [(i, i + by) for i in range(devices) if 0 <= i + by < devices]
    return lax.ppermute(shard, axis, pairs)


def filter_rows(first_idx, n_rows, n_cols):
    row_pos = first_idx + jnp.arange(n_rows, dtype=jnp.int32)
    col_pos = jnp.arange(n_cols, dtype=jnp.int32)
    delta = row_pos[:, None] - col_pos[None, :]
    modes = 2 * (n_cols // 4) + 1
    turned = jnp.mod(modes * delta, 2 * n_cols)
    safe_delta = jnp.where(delta == 0, 1, delta)
    upper = jnp.sin(math.pi * turned.astype(jnp.float32) / n_cols)
    lower = n_cols * jnp.sin(math.pi * safe_delta.astype(jnp.float32) / n_cols)
    band = jnp.where(delta == 0, modes / n_cols, upper / lower)
    return (0.7 * band + jnp.where(delta == 0, 0.3, 0.0)).astype(jnp.bfloat16)


def face_x(planes, direction):
    return shifted(planes, "gx", direction)


def face_y(planes, direction):
    return passed_along(planes, "gy", direction)


def ahead_z(comp):
    zeros = jnp.zeros_like(comp[:1])
    return jnp.concatenate([comp[1:], zeros], axis=0) - comp


def behind_z(comp):
    zeros = jnp.zeros_like(comp[:1])
    return comp - jnp.concatenate([zeros, comp[:-1]], axis=0)


def ahead_x(comp, edge_col):
    return jnp.concatenate([comp[:, :, 1:], edge_col[:, :, None]], axis=2) - comp


def behind_x(comp, edge_col):
    return comp - jnp.concatenate([edge_col[:, :, None], comp[:, :, :-1]], axis=2)


def ahead_y(comp, edge_row):
    return jnp.concatenate([comp[:, 1:, :], edge_row[:, None, :]], axis=1) - comp


def behind_y(comp, edge_row):
    return comp - jnp.concatenate([edge_row[:, None, :], comp[:, :-1, :]], axis=1)


def curl_of_e(e_field):
    next_x = face_x(e_field[1:3, :, :, 0], -1)
    next_y = face_y(jnp.stack([e_field[0, :, 0, :], e_field[2, :, 0, :]]), -1)
    e_x, e_y, e_z = (e_field[0], e_field[1], e_field[2])
    curl_x = ahead_y(e_z, next_y[1]) - ahead_z(e_y)
    curl_y = ahead_z(e_x) - ahead_x(e_z, next_x[1])
    curl_z = ahead_x(e_y, next_x[0]) - ahead_y(e_x, next_y[0])
    return jnp.stack([curl_x, curl_y, curl_z])


def curl_of_h(h_field):
    last_col = h_field.shape[3] - 1
    last_row = h_field.shape[2] - 1
    prev_x = face_x(h_field[1:3, :, :, last_col], 1)
    prev_y = face_y(jnp.stack([h_field[0, :, last_row, :], h_field[2, :, last_row, :]]), 1)
    h_x, h_y, h_z = (h_field[0], h_field[1], h_field[2])
    curl_x = behind_y(h_z, prev_y[1]) - behind_z(h_y)
    curl_y = behind_z(h_x) - behind_x(h_z, prev_x[1])
    curl_z = behind_x(h_y, prev_x[0]) - behind_y(h_x, prev_y[0])
    return jnp.stack([curl_x, curl_y, curl_z])


def smooth(field_in, wire_layers):
    block_rows = field_in.shape[2]
    n_lines = block_rows * lax.axis_size("gy")
    rounded = field_in.astype(jnp.bfloat16)
    f_rows = filter_rows(lax.axis_index("gy") * block_rows, block_rows, n_lines)
    filtered = jnp.einsum(
        "mn,cznx->czmx",
        f_rows,
        lax.all_gather(rounded, "gy", axis=2, tiled=True),
        preferred_element_type=jnp.float32,
    )
    return jnp.where(wire_layers[None, :, None, None] == 1, filtered, field_in)


def body(e_field, h_field, material, permittivity, conductivity, wire_layers):
    h_half = h_field - TIME_STEP * curl_of_e(e_field)
    h_next = smooth(h_half, wire_layers)
    ratio_tab = conductivity * TIME_STEP / (2.0 * permittivity)
    decay_tab = (1.0 - ratio_tab) / (1.0 + ratio_tab)
    gain_tab = TIME_STEP / permittivity / (1.0 + ratio_tab)
    labels = jnp.arange(permittivity.shape[0], dtype=jnp.int32)
    onehot = (material[None] == labels[:, None, None, None]).astype(jnp.float32)
    decay = jnp.sum(onehot * decay_tab[:, None, None, None], axis=0)
    gain = jnp.sum(onehot * gain_tab[:, None, None, None], axis=0)
    e_half = decay[None] * e_field + gain[None] * curl_of_h(h_next)
    e_next = smooth(e_half, wire_layers)
    return (e_next, h_next)


def solution(mesh):
    placed = (
        P(None, None, "gy", "gx"),
        P(None, None, "gy", "gx"),
        P(None, "gy", "gx"),
        P(),
        P(),
        P(),
    )
    return jax.shard_map(
        body,
        mesh=mesh,
        in_specs=placed,
        out_specs=(P(None, None, "gy", "gx"), P(None, None, "gy", "gx")),
        check_vma=False,
    )
```

profile of v0, /device:TPU:1, one launch (start us, length us, event | category | flops | bytes accessed | tf_op | source)
XLA Modules:
  0.0 241.9 jit_solution(864559225283043199)
XLA Ops:
  7.2 0.0 copy-start.4
  7.2 0.0 copy-start.3
  7.2 0.0 copy-start.2
  7.2 0.0 copy-start.5
  7.2 0.0 all-gather.3.cloned.1.call-start
  7.2 0.8 fusion.61
  8.1 8.7 %collective-permute-start = (f32[2,8,128]{2,1,0:T(8,128)S(1)}, f32[2,8,128]{2,1,0:T(8,128)S(1)}, u32[]{:S(2)}, u32[]{:S(2)}) collective-permute-start(f32[2,8,128]{2,1,0:T(8,128)S(1)} %pad_maximum_fusion), channel_id=1, source_target_pairs={{1,0},{2,1},{3,2},{4,3},{5,4},{6,5},{7,6},{8,7},{9,8},{10,9},{11,1... | collective-permute-start | bytes 24584 | tf_op jit(solution)/shard_map/ppermute | solution.py:20
  16.8 1.1 slice.124
  17.9 0.2 copy.62
  18.1 8.2 %collective-permute-start.1 = (f32[2,8,64]{2,1,0:T(8,128)S(1)}, f32[2,8,64]{2,1,0:T(8,128)S(1)}, u32[]{:S(2)}, u32[]{:S(2)}) collective-permute-start(f32[2,8,64]{2,1,0:T(8,128)S(1)} %bitcast.109), channel_id=1, source_target_pairs={{0,480},{32,0},{64,32},{96,64},{128,96},{160,128},{192,160},{224,1... | collective-permute-start | bytes 12296 | tf_op jit(solution)/shard_map/ppermute | solution.py:14
  26.3 1.1 slice_bitcast_fusion.13
  27.4 1.1 slice_bitcast_fusion.8
  28.5 0.1 slice_bitcast_fusion.4
  28.6 0.0 collective-permute-done.1
  28.7 0.1 copy.52
  28.8 0.2 copy.53
  29.0 0.0 collective-permute-done
  29.0 1.3 slice_bitcast_fusion.5
  30.3 0.1 slice.150
  30.4 1.3 fusion.19
  31.7 2.0 fusion.36
  33.7 0.0 all-gather.3.cloned.1.call-update
  33.7 0.0 all-gather.5.cloned.1.call-start
  33.8 0.0 copy-done.4
  33.8 0.0 copy-done.3
  33.8 0.0 copy-done.2
  33.9 0.4 select_reduce_fusion.1
  34.3 0.0 copy-done.5
  34.3 0.0 copy-start
  34.3 83.4 %all-gather.3.cloned.1.call-done = bf16[3,8,2048,128]{3,2,1,0:T(8,128)(2,1)} async-done(((bf16[3,8,64,128]{3,2,1,0:T(8,128)(2,1)}), bf16[3,8,2048,128]{3,2,1,0:T(8,128)(2,1)}) %all-gather.3.cloned.1.call-update) | async-done | bytes 12582928 | tf_op jit(solution)/shard_map/all_gather | solution.py:100
  117.8 9.3 %fusion.1 = f32[3,8,64,128]{3,2,1,0:T(8,128)S(1)} fusion(bf16[3,8,2048,128]{3,2,1,0:T(8,128)(2,1)} %all-gather.3.cloned.1.call-done, pred[8]{0:T(512)(128)(4,1)S(1)} %broadcast_compare_fusion, s32[64]{0:T(128)S(1)} %iota_add_fusion, f32[3,8,64,128]{3,2,1,0:T(8,128)} %param.7, f32[1,8,64,128]{3,2,1,0:T(8,128)S(1)} %get-tuple-element.21, ...), kind=kOutput, calls=%fused_computation.6 | convolution fusion | flops 809697280 | bytes 14942472 | tf_op jit(solution)/shard_map/mn,cznx->czmx/dot_general | solution.py:97
  127.0 0.0 copy-start.1
  127.0 0.4 slice_reduce_fusion
  127.5 0.8 slice_bitcast_fusion.11
  128.3 3.1 %collective-permute-start.2 = (f32[2,8,128]{2,1,0:T(8,128)S(1)}, f32[2,8,128]{2,1,0:T(8,128)S(1)}, u32[]{:S(2)}, u32[]{:S(2)}) collective-permute-start(f32[2,8,128]{2,1,0:T(8,128)S(1)} %pad_maximum_fusion.1), channel_id=1, source_target_pairs={{0,1},{1,2},{2,3},{3,4},{4,5},{5,6},{6,7},{7,8},{8,9},{9,10},{10,1... | collective-permute-start | bytes 24584 | tf_op jit(solution)/shard_map/ppermute | solution.py:20
  131.5 6.0 %collective-permute-start.3 = (f32[2,8,64]{2,1,0:T(8,128)S(1)}, f32[2,8,64]{2,1,0:T(8,128)S(1)}, u32[]{:S(2)}, u32[]{:S(2)}) collective-permute-start(f32[2,8,64]{2,1,0:T(8,128)S(1)} %slice_reduce_fusion), channel_id=1, source_target_pairs={{0,32},{32,64},{64,96},{96,128},{128,160},{160,192},{192,224},{224... | collective-permute-start | bytes 12296 | tf_op jit(solution)/shard_map/ppermute | solution.py:14
  137.6 4.4 %collective-permute-done.3 = f32[2,8,64]{2,1,0:T(8,128)S(1)} collective-permute-done((f32[2,8,64]{2,1,0:T(8,128)S(1)}, f32[2,8,64]{2,1,0:T(8,128)S(1)}, u32[]{:S(2)}, u32[]{:S(2)}) %collective-permute-start.3) | collective-permute-done | bytes 4128 | tf_op jit(solution)/shard_map/ppermute | solution.py:14
  141.9 0.2 copy.57
  142.1 0.2 copy.58
  142.3 0.0 collective-permute-done.2
  142.3 0.2 slice_bitcast_fusion.2
  142.4 1.2 fusion.24
  143.7 0.0 copy-done
  143.7 0.9 fusion.59
  144.6 0.0 all-gather.5.cloned.1.call-update
  144.7 80.4 %all-gather.5.cloned.1.call-done = bf16[3,8,2048,128]{3,2,1,0:T(8,128)(2,1)} async-done(((bf16[3,8,64,128]{3,2,1,0:T(8,128)(2,1)}), bf16[3,8,2048,128]{3,2,1,0:T(8,128)(2,1)}) %all-gather.5.cloned.1.call-update) | async-done | bytes 12582928 | tf_op jit(solution)/shard_map/all_gather | solution.py:100
  225.1 10.0 %fusion = f32[3,8,64,128]{3,2,1,0:T(8,128)} fusion(bf16[3,8,2048,128]{3,2,1,0:T(8,128)(2,1)} %all-gather.5.cloned.1.call-done, pred[8]{0:T(512)(128)(4,1)S(1)} %broadcast_compare_fusion, s32[64]{0:T(128)S(1)} %iota_add_fusion, f32[1,8,64,128]{3,2,1,0:T(8,128)S(1)} %get-tuple-element.11, f32[1,8,64,128]{3,2,1,0:T(8,128)S(1)} %get-tuple-element.7, ...), kind=kOutput, calls=%fused_computation.4 | convolution fusion | flops 809893888 | bytes 15466760 | tf_op jit(solution)/shard_map/mn,cznx->czmx/dot_general | solution.py:97
  235.1 0.0 copy-done.1
  (16 shorter events, 0.2 us)
Async XLA Ops:
  7.2 26.6 %copy-start.4 = (f32[8]{0:T(128)S(1)}, f32[8]{0:T(128)}, u32[]{:S(2)}) copy-start(f32[8]{0:T(128)} %param.10) | copy-start | bytes 100
  7.2 26.6 %copy-start.3 = (f32[8]{0:T(128)S(1)}, f32[8]{0:T(128)}, u32[]{:S(2)}) copy-start(f32[8]{0:T(128)} %param.9) | copy-start | bytes 100
  7.2 26.7 %copy-start.2 = (s32[8,64,128]{2,1,0:T(8,128)S(1)}, s32[8,64,128]{2,1,0:T(8,128)}, u32[]{:S(2)}) copy-start(s32[8,64,128]{2,1,0:T(8,128)} %param.8) | copy-start | bytes 786436
  7.2 27.1 %copy-start.5 = (s32[8]{0:T(128)S(1)}, s32[8]{0:T(128)}, u32[]{:S(2)}) copy-start(s32[8]{0:T(128)} %param.11) | copy-start | bytes 100
  7.2 110.6 %all-gather.3.cloned.1.call-start = ((), (), s32[]{:S(2)}) async-start(), calls=%async_computation | async-start | bytes 12976128 | tf_op jit(solution)/shard_map/all_gather | solution.py:100
  8.1 20.9 %collective-permute-start = (f32[2,8,128]{2,1,0:T(8,128)S(1)}, f32[2,8,128]{2,1,0:T(8,128)S(1)}, u32[]{:S(2)}, u32[]{:S(2)}) collective-permute-start(f32[2,8,128]{2,1,0:T(8,128)S(1)} %pad_maximum_fusion), channel_id=1, source_target_pairs={{1,0},{2,1},{3,2},{4,3},{5,4},{6,5},{7,6},{8,7},{9,8},{10,9},{11,1... | collective-permute-start | bytes 24584 | tf_op jit(solution)/shard_map/ppermute | solution.py:20
  18.1 10.5 %collective-permute-start.1 = (f32[2,8,64]{2,1,0:T(8,128)S(1)}, f32[2,8,64]{2,1,0:T(8,128)S(1)}, u32[]{:S(2)}, u32[]{:S(2)}) collective-permute-start(f32[2,8,64]{2,1,0:T(8,128)S(1)} %bitcast.109), channel_id=1, source_target_pairs={{0,480},{32,0},{64,32},{96,64},{128,96},{160,128},{192,160},{224,1... | collective-permute-start | bytes 12296 | tf_op jit(solution)/shard_map/ppermute | solution.py:14
  33.7 191.3 %all-gather.5.cloned.1.call-start = ((), (), s32[]{:S(2)}) async-start(), calls=%async_computation.1 | async-start | bytes 12976128 | tf_op jit(solution)/shard_map/all_gather | solution.py:100
  34.3 109.4 %copy-start = (f32[3,8,64,128]{3,2,1,0:T(8,128)S(1)}, f32[3,8,64,128]{3,2,1,0:T(8,128)}, u32[]{:S(2)}) copy-start(f32[3,8,64,128]{3,2,1,0:T(8,128)} %param.6) | copy-start | bytes 2359300
  127.0 108.0 %copy-start.1 = (f32[3,8,64,128]{3,2,1,0:T(8,128)}, f32[3,8,64,128]{3,2,1,0:T(8,128)S(1)}, u32[]{:S(2)}) copy-start(f32[3,8,64,128]{3,2,1,0:T(8,128)S(1)} %fusion.1) | copy-start | bytes 2359300
  128.3 13.9 %collective-permute-start.2 = (f32[2,8,128]{2,1,0:T(8,128)S(1)}, f32[2,8,128]{2,1,0:T(8,128)S(1)}, u32[]{:S(2)}, u32[]{:S(2)}) collective-permute-start(f32[2,8,128]{2,1,0:T(8,128)S(1)} %pad_maximum_fusion.1), channel_id=1, source_target_pairs={{0,1},{1,2},{2,3},{3,4},{4,5},{5,6},{6,7},{7,8},{8,9},{9,10},{10,1... | collective-permute-start | bytes 24584 | tf_op jit(solution)/shard_map/ppermute | solution.py:20
  131.5 10.5 %collective-permute-start.3 = (f32[2,8,64]{2,1,0:T(8,128)S(1)}, f32[2,8,64]{2,1,0:T(8,128)S(1)}, u32[]{:S(2)}, u32[]{:S(2)}) collective-permute-start(f32[2,8,64]{2,1,0:T(8,128)S(1)} %slice_reduce_fusion), channel_id=1, source_target_pairs={{0,32},{32,64},{64,96},{96,128},{128,160},{160,192},{192,224},{224... | collective-permute-start | bytes 12296 | tf_op jit(solution)/shard_map/ppermute | solution.py:14
Sparse Core Ops, SparseCore 0:
  33.9 83.8 all-gather.2
  144.8 80.2 all-gather.4
where the time goes:
time: 242 us
  waiting for transfers between devices  168 us (69%)
  starting transfers between devices  26.2 us (11%)
  matrix products  19.2 us (8%)
  between operations  14.4 us (6%)
  other arithmetic  7.32 us (3%)
  local copies, waits for them, and re-layouts  6.5 us (3%)
    all_gather x2, waiting for transfers between devices, smooth(): lax.all_gather(rounded, 'gy', axis=2, tiled=True)  164 us
    dot_general x2, matrix products, smooth(): jnp.einsum('mn,cznx->czmx', f_rows, lax.all_gather(rounded, 'gy', axis=2,...  19.2 us
    ppermute x2, starting transfers between devices, shifted(): return lax.ppermute(value, axis, pairs)  14.2 us
    ppermute x2, starting transfers between devices, passed_along(): return lax.ppermute(shard, axis, pairs)  11.9 us
  transfers between devices with their start and end apart: 6, of which 3 were waited for; matrix products, arithmetic and copies ran while one was open for 2% of the time, Pallas kernels for 0%

commit v1 on v0

--- a/solution.py
+++ b/solution.py
@@ -91,8 +91,17 @@
 
 def smooth(field_in, wire_layers):
     block_rows = field_in.shape[2]
+    n_layers = field_in.shape[1]
+    n_wires = n_layers // 2
     n_lines = block_rows * lax.axis_size("gy")
-    rounded = field_in.astype(jnp.bfloat16)
+    rank = jnp.cumsum(wire_layers) - 1
+    slots = jnp.arange(n_wires, dtype=jnp.int32)
+    picked = (wire_layers[None] == 1) & (rank[None] == slots[:, None])
+    layer_of = jnp.sum(jnp.where(picked, jnp.arange(n_layers, dtype=jnp.int32)[None], 0), axis=1)
+    wires = jnp.concatenate(
+        [lax.dynamic_slice_in_dim(field_in, layer_of[k], 1, axis=1) for k in range(n_wires)], axis=1
+    )
+    rounded = wires.astype(jnp.bfloat16)
     f_rows = filter_rows(lax.axis_index("gy") * block_rows, block_rows, n_lines)
     filtered = jnp.einsum(
         "mn,cznx->czmx",
@@ -100,7 +109,10 @@
         lax.all_gather(rounded, "gy", axis=2, tiled=True),
         preferred_element_type=jnp.float32,
     )
-    return jnp.where(wire_layers[None, :, None, None] == 1, filtered, field_in)
+    out = field_in
+    for k in range(n_wires):
+        out = lax.dynamic_update_slice_in_dim(out, filtered[:, k : k + 1], layer_of[k], axis=1)
+    return out
 
 
 def body(e_field, h_field, material, permittivity, conductivity, wire_layers):

time: 242 us -> 212 us (0.88)
  waiting for transfers between devices: 168 us -> 135 us
  between operations: 14.4 us -> 22.1 us
  matrix products: 19.2 us -> 13.7 us
    all_gather x2, waiting for transfers between devices: 164 us -> 130 us  [smooth(): lax.all_gather(rounded, 'gy', axis=2, tiled=True)]
    dot_general x2, matrix products: 19.2 us -> 13.7 us  [smooth(): jnp.einsum('mn,cznx->czmx', f_rows, lax.all_gather(rounded, 'gy', axis=2,...]
    convert_element_type x2 -> x0, other arithmetic: 2.94 us -> none  [smooth(): rounded = field_in.astype(jnp.bfloat16)]
  transfers between devices with their start and end apart: 6 -> 6, of which waited for: 3 -> 3; matrix products, arithmetic and copies ran while one was open for 2% -> 3% of each run, Pallas kernels for 0% -> 0%
where the time goes in v1:
time: 212 us; the launch traced here: 211 us
  waiting for transfers between devices  135 us (64%)
  starting transfers between devices  26 us (12%)
  between operations  22.1 us (10%)
  matrix products  13.7 us (6%)
  local copies, waits for them, and re-layouts  8.13 us (4%)
  other arithmetic  6.55 us (3%)
    all_gather x2, waiting for transfers between devices, smooth(): lax.all_gather(rounded, 'gy', axis=2, tiled=True)  130 us
    ppermute x2, starting transfers between devices, shifted(): return lax.ppermute(value, axis, pairs)  14 us
    dot_general x2, matrix products, smooth(): jnp.einsum('mn,cznx->czmx', f_rows, lax.all_gather(rounded, 'gy', axis=2,...  13.7 us
    ppermute x2, starting transfers between devices, passed_along(): return lax.ppermute(shard, axis, pairs)  11.9 us
    ppermute x2, waiting for transfers between devices, shifted(): return lax.ppermute(value, axis, pairs)  4.69 us
  transfers between devices with their start and end apart: 6, of which 3 were waited for; matrix products, arithmetic and copies ran while one was open for 3% of the time, Pallas kernels for 0%

profile of v1, /device:TPU:1, one launch (start us, length us, event | category | flops | bytes accessed | tf_op | source)
XLA Modules:
  0.0 211.4 jit_solution(1662647163732602079)
XLA Ops:
  7.2 0.0 copy-start.1
  7.2 0.0 copy-start.3
  7.2 0.0 all-gather.3.cloned.1.call-start
  7.2 0.9 fusion.58
  8.1 8.7 %collective-permute-start = (f32[2,8,128]{2,1,0:T(8,128)S(1)}, f32[2,8,128]{2,1,0:T(8,128)S(1)}, u32[]{:S(2)}, u32[]{:S(2)}) collective-permute-start(f32[2,8,128]{2,1,0:T(8,128)S(1)} %pad_maximum_fusion.2), channel_id=1, source_target_pairs={{1,0},{2,1},{3,2},{4,3},{5,4},{6,5},{7,6},{8,7},{9,8},{10,9},{11,1... | collective-permute-start | bytes 24584 | tf_op jit(solution)/shard_map/ppermute | solution.py:20
  16.9 1.1 slice.172
  18.0 0.2 copy.62
  18.2 0.0 copy-start.4
  18.2 8.3 %collective-permute-start.1 = (f32[2,8,64]{2,1,0:T(8,128)S(1)}, f32[2,8,64]{2,1,0:T(8,128)S(1)}, u32[]{:S(2)}, u32[]{:S(2)}) collective-permute-start(f32[2,8,64]{2,1,0:T(8,128)S(1)} %bitcast.112), channel_id=1, source_target_pairs={{0,480},{32,0},{64,32},{96,64},{128,96},{160,128},{192,160},{224,1... | collective-permute-start | bytes 12296 | tf_op jit(solution)/shard_map/ppermute | solution.py:14
  26.5 1.1 slice_bitcast_fusion.13
  27.6 1.1 slice_bitcast_fusion.8
  28.7 0.7 broadcast_compare_fusion
  29.3 0.8 reduce-window.8
  30.2 0.1 slice_bitcast_fusion.4
  30.3 0.1 select_reduce_fusion.2
  30.4 0.6 fusion.61
  38.7 0.0 collective-permute-done.1
  38.7 0.1 copy.52
  38.9 0.2 copy.53
  39.0 0.0 collective-permute-done
  39.1 1.3 slice_bitcast_fusion.5
  40.3 0.1 slice.210
  40.5 0.2 fusion.17
  40.8 0.1 fusion
  40.9 0.7 pad_maximum_fusion
  41.6 0.0 all-gather.3.cloned.1.call-update
  41.7 0.0 all-gather.5.cloned.1.call-start
  41.8 0.4 select_reduce_fusion.1
  42.2 64.1 %all-gather.3.cloned.1.call-done = bf16[3,4,2048,128]{3,2,1,0:T(8,128)(2,1)} async-done(((bf16[3,4,64,128]{3,2,1,0:T(8,128)(2,1)}), bf16[3,4,2048,128]{3,2,1,0:T(8,128)(2,1)}) %all-gather.3.cloned.1.call-update) | async-done | bytes 6291472 | tf_op jit(solution)/shard_map/all_gather | solution.py:109
  106.3 6.9 %convolution_bitcast_fusion.1 = f32[3,4,64,128]{3,2,1,0:T(8,128)S(1)} fusion(bf16[3,4,2048,128]{3,2,1,0:T(8,128)(2,1)} %all-gather.3.cloned.1.call-done, s32[64]{0:T(128)S(1)} %iota_add_fusion), kind=kOutput, calls=%fused_computation.4 | convolution fusion | flops 406061056 | bytes 6684928 | tf_op jit(solution)/shard_map/mn,cznx->czmx/dot_general | solution.py:106
  113.2 0.0 copy-start
  113.3 0.4 slice_reduce_fusion
  113.7 0.7 slice_bitcast_fusion.11
  114.4 3.2 %collective-permute-start.2 = (f32[2,8,128]{2,1,0:T(8,128)S(1)}, f32[2,8,128]{2,1,0:T(8,128)S(1)}, u32[]{:S(2)}, u32[]{:S(2)}) collective-permute-start(f32[2,8,128]{2,1,0:T(8,128)S(1)} %pad_maximum_fusion.3), channel_id=1, source_target_pairs={{0,1},{1,2},{2,3},{3,4},{4,5},{5,6},{6,7},{7,8},{8,9},{9,10},{10,1... | collective-permute-start | bytes 24584 | tf_op jit(solution)/shard_map/ppermute | solution.py:20
  117.6 5.7 %collective-permute-start.3 = (f32[2,8,64]{2,1,0:T(8,128)S(1)}, f32[2,8,64]{2,1,0:T(8,128)S(1)}, u32[]{:S(2)}, u32[]{:S(2)}) collective-permute-start(f32[2,8,64]{2,1,0:T(8,128)S(1)} %slice_reduce_fusion), channel_id=1, source_target_pairs={{0,32},{32,64},{64,96},{96,128},{128,160},{160,192},{192,224},{224... | collective-permute-start | bytes 12296 | tf_op jit(solution)/shard_map/ppermute | solution.py:14
  123.4 4.7 %collective-permute-done.3 = f32[2,8,64]{2,1,0:T(8,128)S(1)} collective-permute-done((f32[2,8,64]{2,1,0:T(8,128)S(1)}, f32[2,8,64]{2,1,0:T(8,128)S(1)}, u32[]{:S(2)}, u32[]{:S(2)}) %collective-permute-start.3) | collective-permute-done | bytes 4128 | tf_op jit(solution)/shard_map/ppermute | solution.py:14
  128.0 0.2 copy.57
  128.2 0.2 copy.58
  128.4 0.0 collective-permute-done.2
  128.4 0.2 slice_bitcast_fusion.2
  128.6 1.1 fusion.22
  129.7 0.2 fusion.1
  129.9 0.7 pad_maximum_fusion.1
  130.6 0.0 all-gather.5.cloned.1.call-update
  130.6 66.0 %all-gather.5.cloned.1.call-done = bf16[3,4,2048,128]{3,2,1,0:T(8,128)(2,1)} async-done(((bf16[3,4,64,128]{3,2,1,0:T(8,128)(2,1)}), bf16[3,4,2048,128]{3,2,1,0:T(8,128)(2,1)}) %all-gather.5.cloned.1.call-update) | async-done | bytes 6291472 | tf_op jit(solution)/shard_map/all_gather | solution.py:109
  196.7 6.9 %convolution_bitcast_fusion = f32[3,4,64,128]{3,2,1,0:T(8,128)S(1)} fusion(bf16[3,4,2048,128]{3,2,1,0:T(8,128)(2,1)} %all-gather.5.cloned.1.call-done, s32[64]{0:T(128)S(1)} %iota_add_fusion), kind=kOutput, calls=%fused_computation.3 | convolution fusion | flops 406061056 | bytes 6684928 | tf_op jit(solution)/shard_map/mn,cznx->czmx/dot_general | solution.py:106
  203.6 0.0 copy-start.2
  203.6 0.9 copy-done.2
  (34 shorter events, 0.4 us)
Async XLA Ops:
  7.2 33.3 %copy-start.1 = (f32[3,8,64,128]{3,2,1,0:T(8,128)S(1)}, f32[3,8,64,128]{3,2,1,0:T(8,128)}, u32[]{:S(2)}) copy-start(f32[3,8,64,128]{3,2,1,0:T(8,128)} %param.6) | copy-start | bytes 2359300
  7.2 33.6 %copy-start.3 = (f32[3,8,64,128]{3,2,1,0:T(8,128)S(1)}, f32[3,8,64,128]{3,2,1,0:T(8,128)}, u32[]{:S(2)}) copy-start(f32[3,8,64,128]{3,2,1,0:T(8,128)} %param.7) | copy-start | bytes 2359300
  7.2 99.1 %all-gather.3.cloned.1.call-start = ((), (), s32[]{:S(2)}) async-start(), calls=%async_computation | async-start | bytes 6488064 | tf_op jit(solution)/shard_map/all_gather | solution.py:109
  8.1 30.9 %collective-permute-start = (f32[2,8,128]{2,1,0:T(8,128)S(1)}, f32[2,8,128]{2,1,0:T(8,128)S(1)}, u32[]{:S(2)}, u32[]{:S(2)}) collective-permute-start(f32[2,8,128]{2,1,0:T(8,128)S(1)} %pad_maximum_fusion.2), channel_id=1, source_target_pairs={{1,0},{2,1},{3,2},{4,3},{5,4},{6,5},{7,6},{8,7},{9,8},{10,9},{11,1... | collective-permute-start | bytes 24584 | tf_op jit(solution)/shard_map/ppermute | solution.py:20
  18.2 23.6 %copy-start.5 = (f32[8]{0:T(128)S(1)}, f32[8]{0:T(128)}, u32[]{:S(2)}) copy-start(f32[8]{0:T(128)} %param.9) | copy-start | bytes 100
  18.2 23.6 %copy-start.6 = (f32[8]{0:T(128)S(1)}, f32[8]{0:T(128)}, u32[]{:S(2)}) copy-start(f32[8]{0:T(128)} %param.10) | copy-start | bytes 100
  18.2 23.6 %copy-start.4 = (s32[8,64,128]{2,1,0:T(8,128)S(1)}, s32[8,64,128]{2,1,0:T(8,128)}, u32[]{:S(2)}) copy-start(s32[8,64,128]{2,1,0:T(8,128)} %param.8) | copy-start | bytes 786436
  18.2 20.5 %collective-permute-start.1 = (f32[2,8,64]{2,1,0:T(8,128)S(1)}, f32[2,8,64]{2,1,0:T(8,128)S(1)}, u32[]{:S(2)}, u32[]{:S(2)}) collective-permute-start(f32[2,8,64]{2,1,0:T(8,128)S(1)} %bitcast.112), channel_id=1, source_target_pairs={{0,480},{32,0},{64,32},{96,64},{128,96},{160,128},{192,160},{224,1... | collective-permute-start | bytes 12296 | tf_op jit(solution)/shard_map/ppermute | solution.py:14
  41.7 155.0 %all-gather.5.cloned.1.call-start = ((), (), s32[]{:S(2)}) async-start(), calls=%async_computation.1 | async-start | bytes 6488064 | tf_op jit(solution)/shard_map/all_gather | solution.py:109
  113.2 17.4 %copy-start = (f32[3,8,64,128]{3,2,1,0:T(8,128)}, f32[3,8,64,128]{3,2,1,0:T(8,128)S(1)}, u32[]{:S(2)}) copy-start(f32[3,8,64,128]{3,2,1,0:T(8,128)S(1)} %slice_dynamic-update-slice_fusion.4) | copy-start | bytes 2359300
  114.4 13.9 %collective-permute-start.2 = (f32[2,8,128]{2,1,0:T(8,128)S(1)}, f32[2,8,128]{2,1,0:T(8,128)S(1)}, u32[]{:S(2)}, u32[]{:S(2)}) collective-permute-start(f32[2,8,128]{2,1,0:T(8,128)S(1)} %pad_maximum_fusion.3), channel_id=1, source_target_pairs={{0,1},{1,2},{2,3},{3,4},{4,5},{5,6},{6,7},{7,8},{8,9},{9,10},{10,1... | collective-permute-start | bytes 24584 | tf_op jit(solution)/shard_map/ppermute | solution.py:20
  117.6 10.4 %collective-permute-start.3 = (f32[2,8,64]{2,1,0:T(8,128)S(1)}, f32[2,8,64]{2,1,0:T(8,128)S(1)}, u32[]{:S(2)}, u32[]{:S(2)}) collective-permute-start(f32[2,8,64]{2,1,0:T(8,128)S(1)} %slice_reduce_fusion), channel_id=1, source_target_pairs={{0,32},{32,64},{64,96},{96,128},{128,160},{160,192},{192,224},{224... | collective-permute-start | bytes 12296 | tf_op jit(solution)/shard_map/ppermute | solution.py:14
  203.6 0.9 copy-start.2
Sparse Core Ops, SparseCore 0:
  41.8 64.4 all-gather.2
  130.8 65.8 all-gather.4

commit v2 on v0

v2 whole, which is shorter than its diff:
```python
import functools
import math

import jax
import jax.numpy as jnp
import ml_dtypes
import numpy as np
from jax import lax
from jax.experimental import pallas as pl
from jax.experimental.pallas import tpu as pltpu
from jax.sharding import PartitionSpec as P

TIME_STEP = 0.9
MESH = pl.DeviceIdType.MESH
F32 = jnp.float32
BF16 = jnp.bfloat16
TILE = 256


def filter_strip(n_cols, tile):
    row_pos = np.arange(tile, dtype=np.int64)[:, None]
    col_pos = np.arange(2 * n_cols - tile, dtype=np.int64)[None, :]
    delta = row_pos - col_pos + (n_cols - tile)
    modes = 2 * (n_cols // 4) + 1
    turned = np.mod(modes * delta, 2 * n_cols)
    safe_delta = np.where(delta == 0, 1, delta)
    pi = np.float32(math.pi)
    upper = np.sin(pi * turned.astype(np.float32) / np.float32(n_cols))
    lower = np.float32(n_cols) * np.sin(pi * safe_delta.astype(np.float32) / np.float32(n_cols))
    band = np.where(delta == 0, np.float32(modes / n_cols), upper / lower)
    out = np.float32(0.7) * band + np.where(delta == 0, np.float32(0.3), np.float32(0.0))
    return out.astype(np.float32).astype(ml_dtypes.bfloat16)


def owner_of(plane):
    run = plane // 3
    spot = plane % 3 + 1 - run % 2
    return (run * 4 + spot) * 2 + plane % 2


def kernel(
    n_gx, n_gy, n_wires,
    eps_ref, sig_ref, wire_ref, e_ref, h_ref, mat_ref, strip_hbm,
    e_out, h_out,
    strip, xsend, xrecv, ysend, yrecv, wires, lines, res, filt, decay, gain,
    halo_send, halo_recv, wire_send, line_recv, res_send, ret_recv, strip_sem,
):
    _, nz, rows, cols = e_ref.shape
    n_planes = 3 * n_wires
    n_lines = n_gy * rows
    blocks = n_lines // TILE
    per_block = TILE // rows
    gx = lax.axis_index("gx")
    gy = lax.axis_index("gy")

    barrier = pltpu.get_barrier_semaphore()
    for step in (1, n_gx - 1):
        pl.semaphore_signal(
            barrier, inc=1, device_id={"gx": lax.rem(gx + step, n_gx)}, device_id_type=MESH
        )

    def greet(k, _):
        pl.semaphore_signal(
            barrier, inc=1, device_id={"gy": lax.rem(gy + k, n_gy)}, device_id_type=MESH
        )
        return 0

    lax.fori_loop(1, n_gy, greet, 0)

    strip_copy = pltpu.make_async_copy(strip_hbm, strip, strip_sem)
    strip_copy.start()

    lane = lax.broadcasted_iota(jnp.int32, (rows, cols), 1)
    row = lax.broadcasted_iota(jnp.int32, (rows, cols), 0)

    is_wire = [wire_ref[z] for z in range(nz)]
    rank, layer_of, seen = [], [jnp.int32(0)] * n_wires, jnp.int32(0)
    for z in range(nz):
        rank.append(jnp.minimum(seen, n_wires - 1))
        for k in range(n_wires):
            layer_of[k] = layer_of[k] + jnp.where((is_wire[z] == 1) & (seen == k), z, 0)
        seen = seen + is_wire[z]

    def pack_edges(phase, src, col, edge_row):
        total = jnp.zeros((rows, cols), F32)
        for c in (1, 2):
            for z in range(nz):
                j = (c - 1) * nz + z
                moved = pltpu.roll(src[c, z], (j - col) % cols, 1)
                total = jnp.where(lane == j, moved, total)
        xsend[phase] = total
        for i, c in enumerate((0, 2)):
            for z in range(nz):
                ysend[phase, i * nz + z : i * nz + z + 1, :] = src[c, z, edge_row : edge_row + 1, :]

    def halo_copies(phase, step):
        x_copy = pltpu.make_async_remote_copy(
            src_ref=xsend.at[phase],
            dst_ref=xrecv.at[phase],
            send_sem=halo_send.at[phase, 0],
            recv_sem=halo_recv.at[phase, 0],
            device_id={"gx": lax.rem(gx + step + n_gx, n_gx)},
            device_id_type=MESH,
        )
        y_copy = pltpu.make_async_remote_copy(
            src_ref=ysend.at[phase],
            dst_ref=yrecv.at[phase],
            send_sem=halo_send.at[phase, 1],
            recv_sem=halo_recv.at[phase, 1],
            device_id={"gy": lax.rem(gy + step + n_gy, n_gy)},
            device_id_type=MESH,
        )
        return x_copy, y_copy

    def start_halo(phase, step):
        x_copy, y_copy = halo_copies(phase, step)
        x_copy.start()
        sender = gy > 0 if step < 0 else gy < n_gy - 1

        @pl.when(sender)
        def _():
            y_copy.start()

    def finish_halo(phase, step):
        x_copy, y_copy = halo_copies(phase, step)
        x_copy.wait()
        sender = gy > 0 if step < 0 else gy < n_gy - 1
        receiver = gy < n_gy - 1 if step < 0 else gy > 0

        @pl.when(sender)
        def _():
            y_copy.wait_send()

        @pl.when(receiver)
        def _():
            y_copy.wait_recv()

    def start_wires(phase, src):
        for c in range(3):
            for k in range(n_wires):
                wires[phase, c * n_wires + k] = src[c, layer_of[k]].astype(BF16)

        def send(t, _):
            plane = lax.rem(t + gy, n_planes)
            owner = owner_of(plane)

            @pl.when(owner != gy)
            def _():
                pltpu.make_async_remote_copy(
                    src_ref=wires.at[phase, plane],
                    dst_ref=lines.at[phase, gy],
                    send_sem=wire_send.at[phase, plane],
                    recv_sem=line_recv.at[phase, gy],
                    device_id={"gy": owner},
                    device_id_type=MESH,
                ).start()

            @pl.when(owner == gy)
            def _():
                pltpu.make_async_copy(
                    wires.at[phase, plane], lines.at[phase, gy], line_recv.at[phase, gy]
                ).start()

            return 0

        lax.fori_loop(0, n_planes, send, 0)

    chip = gy // 2
    run = chip // 4
    spot = chip % 4 - 1 + run % 2
    my_plane = run * 3 + jnp.clip(spot, 0, 2)
    i_own = owner_of(my_plane) == gy

    def filter_lines(phase):
        @pl.when(i_own)
        def _():
            def arrive(s, _):
                @pl.when(s != gy)
                def _():
                    pltpu.make_async_remote_copy(
                        src_ref=wires.at[phase, my_plane],
                        dst_ref=lines.at[phase, s],
                        send_sem=wire_send.at[phase, my_plane],
                        recv_sem=line_recv.at[phase, s],
                        device_id={"gy": s},
                        device_id_type=MESH,
                    ).wait_recv()

                @pl.when(s == gy)
                def _():
                    pltpu.make_async_copy(
                        wires.at[phase, my_plane], lines.at[phase, s], line_recv.at[phase, s]
                    ).wait()

                return 0

            lax.fori_loop(0, n_gy, arrive, 0)
            if phase == 0:
                strip_copy.wait()

            def block(t, _):
                at = lax.rem(t + my_plane, blocks)
                start = pl.multiple_of((blocks - 1 - at) * TILE, TILE)
                out = jnp.dot(
                    strip[:, pl.ds(start, n_lines)],
                    lines[phase].reshape(n_lines, cols),
                    preferred_element_type=F32,
                )
                res[phase, pl.ds(at * per_block, per_block)] = out.reshape(per_block, rows, cols)

                def give(i, _):
                    to = at * per_block + i

                    @pl.when(to != gy)
                    def _():
                        pltpu.make_async_remote_copy(
                            src_ref=res.at[phase, to],
                            dst_ref=filt.at[phase, my_plane],
                            send_sem=res_send.at[phase, to],
                            recv_sem=ret_recv.at[phase, my_plane],
                            device_id={"gy": to},
                            device_id_type=MESH,
                        ).start()

                    @pl.when(to == gy)
                    def _():
                        pltpu.make_async_copy(
                            res.at[phase, to], filt.at[phase, my_plane], ret_recv.at[phase, my_plane]
                        ).start()

                    return 0

                lax.fori_loop(0, per_block, give, 0)
                return 0

            lax.fori_loop(0, blocks, block, 0)

    def back(phase):
        def arrive(plane, _):
            owner = owner_of(plane)

            @pl.when(owner != gy)
            def _():
                pltpu.make_async_remote_copy(
                    src_ref=res.at[phase, gy],
                    dst_ref=filt.at[phase, plane],
                    send_sem=res_send.at[phase, gy],
                    recv_sem=ret_recv.at[phase, plane],
                    device_id={"gy": owner},
                    device_id_type=MESH,
                ).wait_recv()

            @pl.when(owner == gy)
            def _():
                pltpu.make_async_copy(
                    res.at[phase, gy], filt.at[phase, plane], ret_recv.at[phase, plane]
                ).wait()

            return 0

        lax.fori_loop(0, n_planes, arrive, 0)

    def drain(phase):
        def wire_gone(plane, _):
            owner = owner_of(plane)

            @pl.when(owner != gy)
            def _():
                pltpu.make_async_remote_copy(
                    src_ref=wires.at[phase, plane],
                    dst_ref=lines.at[phase, gy],
                    send_sem=wire_send.at[phase, plane],
                    recv_sem=line_recv.at[phase, gy],
                    device_id={"gy": owner},
                    device_id_type=MESH,
                ).wait_send()

            return 0

        lax.fori_loop(0, n_planes, wire_gone, 0)

        @pl.when(i_own)
        def _():
            def row_gone(to, _):
                @pl.when(to != gy)
                def _():
                    pltpu.make_async_remote_copy(
                        src_ref=res.at[phase, to],
                        dst_ref=filt.at[phase, my_plane],
                        send_sem=res_send.at[phase, to],
                        recv_sem=ret_recv.at[phase, my_plane],
                        device_id={"gy": to},
                        device_id_type=MESH,
                    ).wait_send()

                return 0

            lax.fori_loop(0, n_gy, row_gone, 0)

    def merge(phase, dst):
        for z in range(nz):
            chosen = jnp.full((rows, cols), is_wire[z], jnp.int32) == 1
            for c in range(3):
                dst[c, z] = jnp.where(chosen, filt[phase, c * n_wires + rank[z]], dst[c, z])

    pack_edges(0, e_ref, 0, 0)

    @pl.when(gy == n_gy - 1)
    def _():
        yrecv[0] = jnp.zeros((2 * nz, cols), F32)

    @pl.when(gy == 0)
    def _():
        yrecv[1] = jnp.zeros((2 * nz, cols), F32)

    pl.semaphore_wait(barrier, n_gy + 1)
    start_halo(0, -1)

    tables = []
    for m in range(eps_ref.shape[0]):
        eps = jnp.full((8, cols), eps_ref[m], F32)
        ratio = jnp.full((8, cols), sig_ref[m], F32) * TIME_STEP / (2.0 * eps)
        tables.append(((1.0 - ratio) / (1.0 + ratio), TIME_STEP / eps / (1.0 + ratio)))

    def spread(z, _):
        kind = mat_ref[z].reshape(rows // 8, 8, cols)
        dec = jnp.broadcast_to(tables[0][0][None], kind.shape)
        gai = jnp.broadcast_to(tables[0][1][None], kind.shape)
        for m in range(1, len(tables)):
            hit = kind == m
            dec = jnp.where(hit, tables[m][0][None], dec)
            gai = jnp.where(hit, tables[m][1][None], gai)
        decay[z] = dec.reshape(rows, cols)
        gain[z] = gai.reshape(rows, cols)
        return 0

    lax.fori_loop(0, nz, spread, 0)
    finish_halo(0, -1)

    for z in range(nz):
        ex, ey, ez = e_ref[0, z], e_ref[1, z], e_ref[2, z]
        if z + 1 < nz:
            dz_x, dz_y = e_ref[0, z + 1] - ex, e_ref[1, z + 1] - ey
        else:
            dz_x, dz_y = -ex, -ey
        edge = xrecv[0]

        def ahead_x(comp, j):
            far = jnp.where(
                lane == cols - 1, pltpu.roll(edge, (cols - 1 - j) % cols, 1), pltpu.roll(comp, cols - 1, 1)
            )
            return far - comp

        def ahead_y(comp, j):
            halo = jnp.broadcast_to(yrecv[0, j : j + 1, :], (rows, cols))
            return jnp.where(row == rows - 1, halo, pltpu.roll(comp, rows - 1, 0)) - comp

        curl = (
            ahead_y(ez, nz + z) - dz_y,
            dz_x - ahead_x(ez, nz + z),
            ahead_x(ey, z) - ahead_y(ex, z),
        )
        for c in range(3):
            h_out[c, z] = h_ref[c, z] - TIME_STEP * curl[c]

    start_wires(0, h_out)
    filter_lines(0)
    back(0)
    merge(0, h_out)

    pack_edges(1, h_out, cols - 1, rows - 1)
    start_halo(1, 1)
    finish_halo(1, 1)

    for z in range(nz):
        hx, hy, hz = h_out[0, z], h_out[1, z], h_out[2, z]
        if z > 0:
            dz_x, dz_y = hx - h_out[0, z - 1], hy - h_out[1, z - 1]
        else:
            dz_x, dz_y = hx, hy
        edge = xrecv[1]

        def behind_x(comp, j):
            far = jnp.where(lane == 0, pltpu.roll(edge, (cols - j) % cols, 1), pltpu.roll(comp, 1, 1))
            return comp - far

        def behind_y(comp, j):
            halo = jnp.broadcast_to(yrecv[1, j : j + 1, :], (rows, cols))
            return comp - jnp.where(row == 0, halo, pltpu.roll(comp, 1, 0))

        curl = (
            behind_y(hz, nz + z) - dz_y,
            dz_x - behind_x(hz, nz + z),
            behind_x(hy, z) - behind_y(hx, z),
        )
        for c in range(3):
            e_out[c, z] = decay[z] * e_ref[c, z] + gain[z] * curl[c]

    start_wires(1, e_out)
    filter_lines(1)
    back(1)
    merge(1, e_out)
    drain(0)
    drain(1)

    @pl.when(jnp.logical_not(i_own))
    def _():
        strip_copy.wait()


def body(n_gx, n_gy, e_field, h_field, material, permittivity, conductivity, wire_layers):
    _, nz, rows, cols = e_field.shape
    n_lines = n_gy * rows
    n_wires = nz // 2
    n_planes = 3 * n_wires
    strip = jnp.asarray(filter_strip(n_lines, TILE))
    smem = pl.BlockSpec(memory_space=pltpu.SMEM)
    vmem = pl.BlockSpec(memory_space=pltpu.VMEM)
    block = jax.ShapeDtypeStruct(e_field.shape, F32)
    dma = pltpu.SemaphoreType.DMA
    return pl.pallas_call(
        functools.partial(kernel, n_gx, n_gy, n_wires),
        out_shape=(block, block),
        in_specs=[smem, smem, smem, vmem, vmem, vmem, pl.BlockSpec(memory_space=pl.ANY)],
        out_specs=(vmem, vmem),
        scratch_shapes=[
            pltpu.VMEM(strip.shape, BF16),
            pltpu.VMEM((2, rows, cols), F32),
            pltpu.VMEM((2, rows, cols), F32),
            pltpu.VMEM((2, 2 * nz, cols), F32),
            pltpu.VMEM((2, 2 * nz, cols), F32),
            pltpu.VMEM((2, n_planes, rows, cols), BF16),
            pltpu.VMEM((2, n_gy, rows, cols), BF16),
            pltpu.VMEM((2, n_gy, rows, cols), F32),
            pltpu.VMEM((2, n_planes, rows, cols), F32),
            pltpu.VMEM((nz, rows, cols), F32),
            pltpu.VMEM((nz, rows, cols), F32),
            dma((2, 2)),
            dma((2, 2)),
            dma((2, n_planes)),
            dma((2, n_gy)),
            dma((2, n_gy)),
            dma((2, n_planes)),
            dma,
        ],
        compiler_params=pltpu.CompilerParams(collective_id=0, has_side_effects=True),
    )(permittivity, conductivity, wire_layers, e_field, h_field, material, strip)


def solution(mesh):
    field = P(None, None, "gy", "gx")
    placed = (field, field, P(None, "gy", "gx"), P(), P(), P())
    return jax.shard_map(
        functools.partial(body, mesh.shape["gx"], mesh.shape["gy"]),
        mesh=mesh,
        in_specs=placed,
        out_specs=(field, field),
        check_vma=False,
    )
```

time: 242 us -> 76 us (0.31)
  waiting for transfers between devices: 168 us -> 0 us
  Pallas kernels: 0 us -> 72.1 us
  starting transfers between devices: 26.2 us -> 0 us
  matrix products: 19.2 us -> 0 us
  between operations: 14.4 us -> 0.65 us
  other arithmetic: 7.32 us -> 0 us
  local copies, waits for them, and re-layouts: 6.5 us -> 3.04 us
    all_gather x2 -> x0, waiting for transfers between devices: 164 us -> none  [smooth(): lax.all_gather(rounded, 'gy', axis=2, tiled=True)]
    pallas_call x0 -> x1, Pallas kernels: none -> 72.1 us  [body(): pl.pallas_call(functools.partial(kernel, n_gx, n_gy, n_wires), out_shape=...]
    ppermute x4 -> x0, starting transfers between devices: 26.1 us -> none  [the longest x2 14.2 us: shifted(): return lax.ppermute(value, axis, pairs)]
    dot_general x2 -> x0, matrix products: 19.2 us -> none  [smooth(): jnp.einsum('mn,cznx->czmx', f_rows, lax.all_gather(rounded, 'gy', axis=2,...]
    ppermute x4 -> x0, waiting for transfers between devices: 4.38 us -> none  [the longest x2 4.38 us: shifted(): return lax.ppermute(value, axis, pairs)]
    slice x10 -> x0, local copies, waits for them, and re-layouts: 4.37 us -> none  [the longest x1 1.08 us: ahead_z(): return jnp.concatenate([comp[1:], zeros], axis=0) - comp]
    convert_element_type x2 -> x0, other arithmetic: 2.94 us -> none  [smooth(): rounded = field_in.astype(jnp.bfloat16)]
    unnamed x13 -> x4, local copies, waits for them, and re-layouts: 0.23 us -> 3.04 us
  transfers between devices with their start and end apart: 6 -> 0, of which waited for: 3 -> 0; matrix products, arithmetic and copies ran while one was open for 2% -> 0% of each run, Pallas kernels for 0% -> 0%
where the time goes in v2:
time: 76 us; the launch traced here: 75.8 us
  Pallas kernels  72.1 us (95%)
  local copies, waits for them, and re-layouts  3.04 us (4%)
    pallas_call x1, Pallas kernels, body(): pl.pallas_call(functools.partial(kernel, n_gx, n_gy, n_wires), out_shape=...  72.1 us
    unnamed x4, local copies, waits for them, and re-layouts  3.04 us

profile of v2, /device:TPU:1, one launch (start us, length us, event | category | flops | bytes accessed | tf_op | source)
XLA Modules:
  0.0 75.8 jit_solution(17899124524446565610)
XLA Ops:
  0.6 72.1 %shard_map.86 = (f32[3,8,64,128]{3,2,1,0:T(8,128)}, f32[3,8,64,128]{3,2,1,0:T(8,128)}) custom-call(f32[8]{0:T(128)} %eps_ref.1, f32[8]{0:T(128)} %sig_ref.1, s32[8]{0:T(128)} %wire_ref.1, f32[3,8,64,128]{3,2,1,0:T(8,128)} %e_ref.1, f32[3,8,64,128]{3,2,1,0:T(8,128)} %h_ref.1, s32[8,64,128]{2,1,0:T(8,128)} %mat_ref.1, bf16[256,3840]{1,0:T(8,128)(2,1)} %constant.2.clone.strip_hbm), custom_call_target="tpu_custom_call" | custom-call | tf_op jit(solution)/shard_map/pallas_call | solution.py:421
  72.8 0.0 copy-start
  72.8 2.2 %copy.11 = f32[3,8,64,128]{3,2,1,0:T(8,128)} copy(f32[3,8,64,128]{3,2,1,0:T(8,128)} %get-tuple-element.4) | data formatting | bytes 1572864
  75.0 0.0 copy-done
  75.0 0.9 %copy.12 = f32[3,8,64,128]{3,2,1,0:T(8,128)} copy(f32[3,8,64,128]{3,2,1,0:T(8,128)S(1)} %copy-done) | data formatting | bytes 1572864
Async XLA Ops:
  72.8 2.2 %copy-start = (f32[3,8,64,128]{3,2,1,0:T(8,128)S(1)}, f32[3,8,64,128]{3,2,1,0:T(8,128)}, u32[]{:S(2)}) copy-start(f32[3,8,64,128]{3,2,1,0:T(8,128)} %get-tuple-element.5) | copy-start | bytes 2359300

commit v3 on v2

--- a/solution.py
+++ b/solution.py
@@ -32,18 +32,27 @@
     return out.astype(np.float32).astype(ml_dtypes.bfloat16)
 
 
-def owner_of(plane):
-    run = plane // 3
-    spot = plane % 3 + 1 - run % 2
-    return (run * 4 + spot) * 2 + plane % 2
+def owner_on(chip):
+    return chip * 2 + (chip + chip // 4) % 2
+
+
+def plane_of(chip):
+    return chip // 4 * 3 + (chip % 4 + 2) % 3
+
+
+def giver_of(plane, gy):
+    far = gy // 4 % 2
+    spot = plane % 3
+    z = jnp.where(spot == 2, 3 * far, spot + 1)
+    return owner_on(plane // 3 * 4 + z)
 
 
 def kernel(
     n_gx, n_gy, n_wires,
-    eps_ref, sig_ref, wire_ref, e_ref, h_ref, mat_ref, strip_hbm,
-    e_out, h_out,
-    strip, xsend, xrecv, ysend, yrecv, wires, lines, res, filt, decay, gain,
-    halo_send, halo_recv, wire_send, line_recv, res_send, ret_recv, strip_sem,
+    eps_ref, sig_ref, wire_ref, e_hbm, h_hbm, mat_hbm, strip_hbm,
+    e_hbm_out, h_hbm_out,
+    e_ref, h_ref, mat_ref, e_out, h_out, strip, xsend, xrecv, ysend, yrecv, wires, lines, res, filt, decay, gain,
+    halo_send, halo_recv, wire_send, line_recv, res_send, ret_recv, strip_sem, in_sem, out_sem,
 ):
     _, nz, rows, cols = e_ref.shape
     n_planes = 3 * n_wires
@@ -52,6 +61,14 @@
     per_block = TILE // rows
     gx = lax.axis_index("gx")
     gy = lax.axis_index("gy")
+
+    n_chips = n_gy // 2
+    inputs = [
+        pltpu.make_async_copy(src, dst, in_sem.at[i])
+        for i, (src, dst) in enumerate(((e_hbm, e_ref), (h_hbm, h_ref), (mat_hbm, mat_ref)))
+    ]
+    for copy in inputs:
+        copy.start()
 
     barrier = pltpu.get_barrier_semaphore()
     for step in (1, n_gx - 1):
@@ -141,15 +158,16 @@
                 wires[phase, c * n_wires + k] = src[c, layer_of[k]].astype(BF16)
 
         def send(t, _):
-            plane = lax.rem(t + gy, n_planes)
-            owner = owner_of(plane)
+            to = lax.rem(t + gy // 2, n_chips)
+            plane = plane_of(to)
+            owner = owner_on(to)
 
             @pl.when(owner != gy)
             def _():
                 pltpu.make_async_remote_copy(
                     src_ref=wires.at[phase, plane],
                     dst_ref=lines.at[phase, gy],
-                    send_sem=wire_send.at[phase, plane],
+                    send_sem=wire_send.at[phase, to],
                     recv_sem=line_recv.at[phase, gy],
                     device_id={"gy": owner},
                     device_id_type=MESH,
@@ -163,13 +181,15 @@
 
             return 0
 
-        lax.fori_loop(0, n_planes, send, 0)
+        lax.fori_loop(0, n_chips, send, 0)
 
     chip = gy // 2
-    run = chip // 4
-    spot = chip % 4 - 1 + run % 2
-    my_plane = run * 3 + jnp.clip(spot, 0, 2)
-    i_own = owner_of(my_plane) == gy
+    my_plane = plane_of(chip)
+    i_own = owner_on(chip) == gy
+    depth = chip % 4
+
+    def serves(at):
+        return (depth == 1) | (depth == 2) | (depth // 2 == at % 2)
 
     def filter_lines(phase):
         @pl.when(i_own)
@@ -180,7 +200,7 @@
                     pltpu.make_async_remote_copy(
                         src_ref=wires.at[phase, my_plane],
                         dst_ref=lines.at[phase, s],
-                        send_sem=wire_send.at[phase, my_plane],
+                        send_sem=wire_send.at[phase, 0],
                         recv_sem=line_recv.at[phase, s],
                         device_id={"gy": s},
                         device_id_type=MESH,
@@ -199,45 +219,49 @@
                 strip_copy.wait()
 
             def block(t, _):
-                at = lax.rem(t + my_plane, blocks)
-                start = pl.multiple_of((blocks - 1 - at) * TILE, TILE)
-                out = jnp.dot(
-                    strip[:, pl.ds(start, n_lines)],
-                    lines[phase].reshape(n_lines, cols),
-                    preferred_element_type=F32,
-                )
-                res[phase, pl.ds(at * per_block, per_block)] = out.reshape(per_block, rows, cols)
-
-                def give(i, _):
-                    to = at * per_block + i
-
-                    @pl.when(to != gy)
-                    def _():
-                        pltpu.make_async_remote_copy(
-                            src_ref=res.at[phase, to],
-                            dst_ref=filt.at[phase, my_plane],
-                            send_sem=res_send.at[phase, to],
-                            recv_sem=ret_recv.at[phase, my_plane],
-                            device_id={"gy": to},
-                            device_id_type=MESH,
-                        ).start()
-
-                    @pl.when(to == gy)
-                    def _():
-                        pltpu.make_async_copy(
-                            res.at[phase, to], filt.at[phase, my_plane], ret_recv.at[phase, my_plane]
-                        ).start()
-
-                    return 0
-
-                lax.fori_loop(0, per_block, give, 0)
+                at = lax.rem(t + chip // 2, blocks)
+
+                @pl.when(serves(at))
+                def _():
+                    start = pl.multiple_of((blocks - 1 - at) * TILE, TILE)
+                    out = jnp.dot(
+                        strip[:, pl.ds(start, n_lines)],
+                        lines[phase].reshape(n_lines, cols),
+                        preferred_element_type=F32,
+                    )
+                    res[phase, pl.ds(at * per_block, per_block)] = out.reshape(per_block, rows, cols)
+
+                    def give(i, _):
+                        to = at * per_block + i
+
+                        @pl.when(to != gy)
+                        def _():
+                            pltpu.make_async_remote_copy(
+                                src_ref=res.at[phase, to],
+                                dst_ref=filt.at[phase, my_plane],
+                                send_sem=res_send.at[phase, to],
+                                recv_sem=ret_recv.at[phase, my_plane],
+                                device_id={"gy": to},
+                                device_id_type=MESH,
+                            ).start()
+
+                        @pl.when(to == gy)
+                        def _():
+                            pltpu.make_async_copy(
+                                res.at[phase, to], filt.at[phase, my_plane], ret_recv.at[phase, my_plane]
+                            ).start()
+
+                        return 0
+
+                    lax.fori_loop(0, per_block, give, 0)
                 return 0
+
 
             lax.fori_loop(0, blocks, block, 0)
 
     def back(phase):
         def arrive(plane, _):
-            owner = owner_of(plane)
+            owner = giver_of(plane, gy)
 
             @pl.when(owner != gy)
             def _():
@@ -261,15 +285,15 @@
         lax.fori_loop(0, n_planes, arrive, 0)
 
     def drain(phase):
-        def wire_gone(plane, _):
-            owner = owner_of(plane)
+        def wire_gone(to, _):
+            owner = owner_on(to)
 
             @pl.when(owner != gy)
             def _():
                 pltpu.make_async_remote_copy(
-                    src_ref=wires.at[phase, plane],
+                    src_ref=wires.at[phase, plane_of(to)],
                     dst_ref=lines.at[phase, gy],
-                    send_sem=wire_send.at[phase, plane],
+                    send_sem=wire_send.at[phase, to],
                     recv_sem=line_recv.at[phase, gy],
                     device_id={"gy": owner},
                     device_id_type=MESH,
@@ -277,12 +301,12 @@
 
             return 0
 
-        lax.fori_loop(0, n_planes, wire_gone, 0)
+        lax.fori_loop(0, n_chips, wire_gone, 0)
 
         @pl.when(i_own)
         def _():
             def row_gone(to, _):
-                @pl.when(to != gy)
+                @pl.when((to != gy) & serves(to // per_block))
                 def _():
                     pltpu.make_async_remote_copy(
                         src_ref=res.at[phase, to],
@@ -303,6 +327,12 @@
             for c in range(3):
                 dst[c, z] = jnp.where(chosen, filt[phase, c * n_wires + rank[z]], dst[c, z])
 
+    results = (
+        pltpu.make_async_copy(h_out, h_hbm_out, out_sem.at[0]),
+        pltpu.make_async_copy(e_out, e_hbm_out, out_sem.at[1]),
+    )
+
+    inputs[0].wait()
     pack_edges(0, e_ref, 0, 0)
 
     @pl.when(gy == n_gy - 1)
@@ -316,6 +346,8 @@
     pl.semaphore_wait(barrier, n_gy + 1)
     start_halo(0, -1)
 
+    inputs[1].wait()
+    inputs[2].wait()
     tables = []
     for m in range(eps_ref.shape[0]):
         eps = jnp.full((8, cols), eps_ref[m], F32)
@@ -370,6 +402,7 @@
 
     pack_edges(1, h_out, cols - 1, rows - 1)
     start_halo(1, 1)
+    results[0].start()
     finish_halo(1, 1)
 
     for z in range(nz):
@@ -400,12 +433,16 @@
     filter_lines(1)
     back(1)
     merge(1, e_out)
+    results[1].start()
     drain(0)
     drain(1)
 
     @pl.when(jnp.logical_not(i_own))
     def _():
         strip_copy.wait()
+
+    for copy in results:
+        copy.wait()
 
 
 def body(n_gx, n_gy, e_field, h_field, material, permittivity, conductivity, wire_layers):
@@ -415,15 +452,20 @@
     n_planes = 3 * n_wires
     strip = jnp.asarray(filter_strip(n_lines, TILE))
     smem = pl.BlockSpec(memory_space=pltpu.SMEM)
-    vmem = pl.BlockSpec(memory_space=pltpu.VMEM)
+    hbm = pl.BlockSpec(memory_space=pl.ANY)
     block = jax.ShapeDtypeStruct(e_field.shape, F32)
     dma = pltpu.SemaphoreType.DMA
     return pl.pallas_call(
         functools.partial(kernel, n_gx, n_gy, n_wires),
         out_shape=(block, block),
-        in_specs=[smem, smem, smem, vmem, vmem, vmem, pl.BlockSpec(memory_space=pl.ANY)],
-        out_specs=(vmem, vmem),
+        in_specs=[smem, smem, smem, hbm, hbm, hbm, hbm],
+        out_specs=(hbm, hbm),
         scratch_shapes=[
+            pltpu.VMEM(e_field.shape, F32),
+            pltpu.VMEM(h_field.shape, F32),
+            pltpu.VMEM(material.shape, jnp.int32),
+            pltpu.VMEM(e_field.shape, F32),
+            pltpu.VMEM(h_field.shape, F32),
             pltpu.VMEM(strip.shape, BF16),
             pltpu.VMEM((2, rows, cols), F32),
             pltpu.VMEM((2, rows, cols), F32),
@@ -437,11 +479,13 @@
             pltpu.VMEM((nz, rows, cols), F32),
             dma((2, 2)),
             dma((2, 2)),
-            dma((2, n_planes)),
+            dma((2, n_gy // 2)),
             dma((2, n_gy)),
             dma((2, n_gy)),
             dma((2, n_planes)),
             dma,
+            dma((3,)),
+            dma((2,)),
         ],
         compiler_params=pltpu.CompilerParams(collective_id=0, has_side_effects=True),
     )(permittivity, conductivity, wire_layers, e_field, h_field, material, strip)

time: 76 us -> 67.4 us (0.89)
  Pallas kernels: 72.1 us -> 63.5 us
    pallas_call x1, Pallas kernels: 72.1 us -> 63.5 us  [body(): pl.pallas_call(functools.partial(kernel, n_gx, n_gy, n_wires), out_shape=...]
where the time goes in v3:
time: 67.4 us; the launch traced here: 67.2 us
  Pallas kernels  63.5 us (94%)
  local copies, waits for them, and re-layouts  3.04 us (5%)
    pallas_call x1, Pallas kernels, body(): pl.pallas_call(functools.partial(kernel, n_gx, n_gy, n_wires), out_shape=...  63.5 us
    unnamed x4, local copies, waits for them, and re-layouts  3.04 us

profile of v3, /device:TPU:1, one launch (start us, length us, event | category | flops | bytes accessed | tf_op | source)
XLA Modules:
  0.0 67.2 jit_solution(10053023457502409205)
XLA Ops:
  0.6 63.5 %shard_map.86 = (f32[3,8,64,128]{3,2,1,0:T(8,128)}, f32[3,8,64,128]{3,2,1,0:T(8,128)}) custom-call(f32[8]{0:T(128)} %eps_ref.1, f32[8]{0:T(128)} %sig_ref.1, s32[8]{0:T(128)} %wire_ref.1, f32[3,8,64,128]{3,2,1,0:T(8,128)} %e_hbm.1, f32[3,8,64,128]{3,2,1,0:T(8,128)} %h_hbm.1, s32[8,64,128]{2,1,0:T(8,128)} %mat_hbm.1, bf16[256,3840]{1,0:T(8,128)(2,1)} %constant.2.clone.strip_hbm), custom_call_target="tpu_custom_call" | custom-call | tf_op jit(solution)/shard_map/pallas_call | solution.py:458
  64.2 0.0 copy-start
  64.2 2.2 %copy.11 = f32[3,8,64,128]{3,2,1,0:T(8,128)} copy(f32[3,8,64,128]{3,2,1,0:T(8,128)} %get-tuple-element.4) | data formatting | bytes 1572864
  66.3 0.0 copy-done
  66.4 0.9 %copy.12 = f32[3,8,64,128]{3,2,1,0:T(8,128)} copy(f32[3,8,64,128]{3,2,1,0:T(8,128)S(1)} %copy-done) | data formatting | bytes 1572864
Async XLA Ops:
  64.2 2.2 %copy-start = (f32[3,8,64,128]{3,2,1,0:T(8,128)S(1)}, f32[3,8,64,128]{3,2,1,0:T(8,128)}, u32[]{:S(2)}) copy-start(f32[3,8,64,128]{3,2,1,0:T(8,128)} %get-tuple-element.5) | copy-start | bytes 2359300

commit v4 on v3

--- a/solution.py
+++ b/solution.py
@@ -40,6 +40,10 @@
     return chip // 4 * 3 + (chip % 4 + 2) % 3
 
 
+def edge_owner(level):
+    return (level * 5) * 2 + 1
+
+
 def giver_of(plane, gy):
     far = gy // 4 % 2
     spot = plane % 3
@@ -52,7 +56,9 @@
     eps_ref, sig_ref, wire_ref, e_hbm, h_hbm, mat_hbm, strip_hbm,
     e_hbm_out, h_hbm_out,
     e_ref, h_ref, mat_ref, e_out, h_out, strip, xsend, xrecv, ysend, yrecv, wires, lines, res, filt, decay, gain,
+    edge_low, edge_lines, edge_res, edge_filt, tails,
     halo_send, halo_recv, wire_send, line_recv, res_send, ret_recv, strip_sem, in_sem, out_sem,
+    edge_send, edge_recv, edge_give, edge_back, tail_send, tail_recv,
 ):
     _, nz, rows, cols = e_ref.shape
     n_planes = 3 * n_wires
@@ -191,6 +197,186 @@
     def serves(at):
         return (depth == 1) | (depth == 2) | (depth // 2 == at % 2)
 
+    def tail_copy(plane, to):
+        return pltpu.make_async_remote_copy(
+            src_ref=res.at[0, to, pl.ds(rows - 8, 8)],
+            dst_ref=tails.at[plane],
+            send_sem=tail_send.at[to],
+            recv_sem=tail_recv.at[plane],
+            device_id={"gy": lax.rem(to + 1, n_gy)},
+            device_id_type=MESH,
+        )
+
+    def own_tail(plane, to):
+        return pltpu.make_async_copy(
+            res.at[0, to, pl.ds(rows - 8, 8)], tails.at[plane], tail_recv.at[plane]
+        )
+
+    has_tails = my_plane // n_wires != 1
+
+    def start_tail(to):
+        @pl.when(has_tails & (to + 1 < n_gy) & (to + 1 != gy))
+        def _():
+            tail_copy(my_plane, to).start()
+
+        @pl.when(has_tails & (to + 1 == gy))
+        def _():
+            own_tail(my_plane, to).start()
+
+    level = chip % 4
+    i_edge = edge_owner(level) == gy
+
+    def edge_copy(to_level, source):
+        return pltpu.make_async_remote_copy(
+            src_ref=edge_low,
+            dst_ref=edge_lines.at[source],
+            send_sem=edge_send.at[to_level],
+            recv_sem=edge_recv.at[source],
+            device_id={"gy": edge_owner(to_level)},
+            device_id_type=MESH,
+        )
+
+    def own_edge():
+        return pltpu.make_async_copy(edge_low, edge_lines.at[gy], edge_recv.at[gy])
+
+    def start_edges():
+        edge_low[...] = xrecv[1].astype(BF16)
+
+        def send(t, _):
+            to_level = lax.rem(t + level, 4)
+
+            @pl.when(edge_owner(to_level) != gy)
+            def _():
+                edge_copy(to_level, gy).start()
+
+            @pl.when(edge_owner(to_level) == gy)
+            def _():
+                own_edge().start()
+
+            return 0
+
+        lax.fori_loop(0, 4, send, 0)
+
+    def edge_give_copy(slot):
+        return pltpu.make_async_remote_copy(
+            src_ref=edge_res.at[slot],
+            dst_ref=edge_filt,
+            send_sem=edge_give.at[slot],
+            recv_sem=edge_back,
+            device_id={"gy": (slot // 2 * 4 + level) * 2 + slot % 2},
+            device_id_type=MESH,
+        )
+
+    def own_edge_give(slot):
+        return pltpu.make_async_copy(edge_res.at[slot], edge_filt, edge_back)
+
+    own_slot = chip // 4 * 2 + gy % 2
+
+    def filter_edges():
+        @pl.when(i_edge)
+        def _():
+            def arrive(s, _):
+                @pl.when(s != gy)
+                def _():
+                    edge_copy(level, s).wait_recv()
+
+                @pl.when(s == gy)
+                def _():
+                    own_edge().wait()
+
+                return 0
+
+            lax.fori_loop(0, n_gy, arrive, 0)
+
+            def block(t, _):
+                run = lax.rem(t + level + 1, n_chips // 4)
+                at = run * 2 + level // 2
+                start = pl.multiple_of((blocks - 1 - at) * TILE, TILE)
+                top = pl.multiple_of(level % 2 * (TILE // 2), TILE // 2)
+                out = jnp.dot(
+                    strip[pl.ds(top, TILE // 2), pl.ds(start, n_lines)],
+                    edge_lines[...].reshape(n_lines, cols),
+                    preferred_element_type=F32,
+                )
+                edge_res[pl.ds(run * 2, 2)] = out.reshape(2, rows, cols)
+
+                def give(i, _):
+                    slot = run * 2 + i
+
+                    @pl.when(slot != own_slot)
+                    def _():
+                        edge_give_copy(slot).start()
+
+                    @pl.when(slot == own_slot)
+                    def _():
+                        own_edge_give(slot).start()
+
+                    return 0
+
+                lax.fori_loop(0, 2, give, 0)
+                return 0
+
+            lax.fori_loop(0, n_chips // 4, block, 0)
+
+    def edges_back():
+        @pl.when(i_edge)
+        def _():
+            own_edge_give(own_slot).wait()
+
+        @pl.when(jnp.logical_not(i_edge))
+        def _():
+            edge_give_copy(own_slot).wait_recv()
+
+        @pl.when(gy > 0)
+        def _():
+            def arrive(t, _):
+                plane = t + t // n_wires * n_wires
+                giver = giver_of(plane, gy - 1)
+
+                @pl.when(giver != gy)
+                def _():
+                    tail_copy(plane, gy).wait_recv()
+
+                @pl.when(giver == gy)
+                def _():
+                    own_tail(plane, gy - 1).wait()
+
+                return 0
+
+            lax.fori_loop(0, 2 * n_wires, arrive, 0)
+
+    def edges_gone():
+        def sent(to_level, _):
+            @pl.when(edge_owner(to_level) != gy)
+            def _():
+                edge_copy(to_level, gy).wait_send()
+
+            return 0
+
+        lax.fori_loop(0, 4, sent, 0)
+
+        @pl.when(i_edge)
+        def _():
+            def given(slot, _):
+                @pl.when(slot != own_slot)
+                def _():
+                    edge_give_copy(slot).wait_send()
+
+                return 0
+
+            lax.fori_loop(0, n_chips // 2, given, 0)
+
+        @pl.when(i_own & has_tails)
+        def _():
+            def tail_gone(to, _):
+                @pl.when((to + 1 != gy) & serves(to // per_block))
+                def _():
+                    tail_copy(my_plane, to).wait_send()
+
+                return 0
+
+            lax.fori_loop(0, n_gy - 1, tail_gone, 0)
+
     def filter_lines(phase):
         @pl.when(i_own)
         def _():
@@ -215,9 +401,6 @@
                 return 0
 
             lax.fori_loop(0, n_gy, arrive, 0)
-            if phase == 0:
-                strip_copy.wait()
-
             def block(t, _):
                 at = lax.rem(t + chip // 2, blocks)
 
@@ -251,6 +434,8 @@
                                 res.at[phase, to], filt.at[phase, my_plane], ret_recv.at[phase, my_plane]
                             ).start()
 
+                        if phase == 0:
+                            start_tail(to)
                         return 0
 
                     lax.fori_loop(0, per_block, give, 0)
@@ -342,6 +527,7 @@
     @pl.when(gy == 0)
     def _():
         yrecv[1] = jnp.zeros((2 * nz, cols), F32)
+        tails[...] = jnp.zeros(tails.shape, F32)
 
     pl.semaphore_wait(barrier, n_gy + 1)
     start_halo(0, -1)
@@ -396,14 +582,22 @@
             h_out[c, z] = h_ref[c, z] - TIME_STEP * curl[c]
 
     start_wires(0, h_out)
+    pack_edges(1, h_out, cols - 1, rows - 1)
+    start_halo(1, 1)
+    finish_halo(1, 1)
+    start_edges()
+    strip_copy.wait()
     filter_lines(0)
+    filter_edges()
     back(0)
     merge(0, h_out)
-
-    pack_edges(1, h_out, cols - 1, rows - 1)
-    start_halo(1, 1)
     results[0].start()
-    finish_halo(1, 1)
+    edges_back()
+
+    kept = jnp.zeros((rows, cols), jnp.int32)
+    for z in range(nz):
+        kept = jnp.where(lane % nz == z, is_wire[z], kept)
+    left = jnp.where(kept == 1, edge_filt[...], xrecv[1])
 
     for z in range(nz):
         hx, hy, hz = h_out[0, z], h_out[1, z], h_out[2, z]
@@ -411,14 +605,15 @@
             dz_x, dz_y = hx - h_out[0, z - 1], hy - h_out[1, z - 1]
         else:
             dz_x, dz_y = hx, hy
-        edge = xrecv[1]
-
         def behind_x(comp, j):
-            far = jnp.where(lane == 0, pltpu.roll(edge, (cols - j) % cols, 1), pltpu.roll(comp, 1, 1))
+            far = jnp.where(lane == 0, pltpu.roll(left, (cols - j) % cols, 1), pltpu.roll(comp, 1, 1))
             return comp - far
 
         def behind_y(comp, j):
-            halo = jnp.broadcast_to(yrecv[1, j : j + 1, :], (rows, cols))
+            plane = (j // nz) * 2 * n_wires + rank[z]
+            raw = jnp.broadcast_to(yrecv[1, j : j + 1, :], (rows, cols))
+            filtered = jnp.broadcast_to(tails[plane][7:8], (rows, cols))
+            halo = jnp.where(jnp.full((rows, cols), is_wire[z], jnp.int32) == 1, filtered, raw)
             return comp - jnp.where(row == 0, halo, pltpu.roll(comp, 1, 0))
 
         curl = (
@@ -435,11 +630,8 @@
     merge(1, e_out)
     results[1].start()
     drain(0)
+    edges_gone()
     drain(1)
-
-    @pl.when(jnp.logical_not(i_own))
-    def _():
-        strip_copy.wait()
 
     for copy in results:
         copy.wait()
@@ -477,6 +669,11 @@
             pltpu.VMEM((2, n_planes, rows, cols), F32),
             pltpu.VMEM((nz, rows, cols), F32),
             pltpu.VMEM((nz, rows, cols), F32),
+            pltpu.VMEM((rows, cols), BF16),
+            pltpu.VMEM((n_gy, rows, cols), BF16),
+            pltpu.VMEM((n_gy // 4, rows, cols), F32),
+            pltpu.VMEM((rows, cols), F32),
+            pltpu.VMEM((n_planes, 8, cols), F32),
             dma((2, 2)),
             dma((2, 2)),
             dma((2, n_gy // 2)),
@@ -486,6 +683,12 @@
             dma,
             dma((3,)),
             dma((2,)),
+            dma((4,)),
+            dma((n_gy,)),
+            dma((n_gy // 4,)),
+            dma,
+            dma((n_gy,)),
+            dma((n_planes,)),
         ],
         compiler_params=pltpu.CompilerParams(collective_id=0, has_side_effects=True),
     )(permittivity, conductivity, wire_layers, e_field, h_field, material, strip)

time: 67.4 us -> 65.4 us (0.970); the launches traced: 67.2 us -> 64.4 us
  Pallas kernels: 63.5 us -> 60.7 us
    pallas_call x1, Pallas kernels: 63.5 us -> 60.7 us  [body(): pl.pallas_call(functools.partial(kernel, n_gx, n_gy, n_wires), out_shape=...]
where the time goes in v4:
time: 65.4 us; the launch traced here: 64.4 us
  Pallas kernels  60.7 us (93%)
  local copies, waits for them, and re-layouts  3.04 us (5%)
    pallas_call x1, Pallas kernels, body(): pl.pallas_call(functools.partial(kernel, n_gx, n_gy, n_wires), out_shape=...  60.7 us
    unnamed x4, local copies, waits for them, and re-layouts  3.04 us

profile of v4, /device:TPU:1, one launch (start us, length us, event | category | flops | bytes accessed | tf_op | source)
XLA Modules:
  0.0 64.4 jit_solution(2231868260700014485)
XLA Ops:
  0.6 60.7 %shard_map.86 = (f32[3,8,64,128]{3,2,1,0:T(8,128)}, f32[3,8,64,128]{3,2,1,0:T(8,128)}) custom-call(f32[8]{0:T(128)} %eps_ref.1, f32[8]{0:T(128)} %sig_ref.1, s32[8]{0:T(128)} %wire_ref.1, f32[3,8,64,128]{3,2,1,0:T(8,128)} %e_hbm.1, f32[3,8,64,128]{3,2,1,0:T(8,128)} %h_hbm.1, s32[8,64,128]{2,1,0:T(8,128)} %mat_hbm.1, bf16[256,3840]{1,0:T(8,128)(2,1)} %constant.2.clone.strip_hbm), custom_call_target="tpu_custom_call" | custom-call | tf_op jit(solution)/shard_map/pallas_call | solution.py:650
  61.3 0.0 copy-start
  61.4 2.2 %copy.11 = f32[3,8,64,128]{3,2,1,0:T(8,128)} copy(f32[3,8,64,128]{3,2,1,0:T(8,128)} %get-tuple-element.4) | data formatting | bytes 1572864
  63.5 0.0 copy-done
  63.5 0.9 %copy.12 = f32[3,8,64,128]{3,2,1,0:T(8,128)} copy(f32[3,8,64,128]{3,2,1,0:T(8,128)S(1)} %copy-done) | data formatting | bytes 1572864
Async XLA Ops:
  61.3 2.2 %copy-start = (f32[3,8,64,128]{3,2,1,0:T(8,128)S(1)}, f32[3,8,64,128]{3,2,1,0:T(8,128)}, u32[]{:S(2)}) copy-start(f32[3,8,64,128]{3,2,1,0:T(8,128)} %get-tuple-element.5) | copy-start | bytes 2359300

commit v5 on v4

--- a/solution.py
+++ b/solution.py
@@ -164,7 +164,7 @@
                 wires[phase, c * n_wires + k] = src[c, layer_of[k]].astype(BF16)
 
         def send(t, _):
-            to = lax.rem(t + gy // 2, n_chips)
+            to = lax.rem(t + 4 + gy // 2, n_chips)
             plane = plane_of(to)
             owner = owner_on(to)
 
@@ -581,9 +581,9 @@
         for c in range(3):
             h_out[c, z] = h_ref[c, z] - TIME_STEP * curl[c]
 
-    start_wires(0, h_out)
     pack_edges(1, h_out, cols - 1, rows - 1)
     start_halo(1, 1)
+    start_wires(0, h_out)
     finish_halo(1, 1)
     start_edges()
     strip_copy.wait()

time: 65.4 us -> 65 us (level)
  no operation moved by 1% of the time
where the time goes in v5:
time: 65 us; the launch traced here: 64.1 us
  Pallas kernels  60.4 us (93%)
  local copies, waits for them, and re-layouts  3.04 us (5%)
  between operations  0.65 us (1%)
    pallas_call x1, Pallas kernels, body(): pl.pallas_call(functools.partial(kernel, n_gx, n_gy, n_wires), out_shape=...  60.4 us
    unnamed x4, local copies, waits for them, and re-layouts  3.04 us

profile of v5, /device:TPU:1, one launch (start us, length us, event | category | flops | bytes accessed | tf_op | source)
XLA Modules:
  0.0 64.1 jit_solution(5366551892423351282)
XLA Ops:
  0.6 60.4 %shard_map.86 = (f32[3,8,64,128]{3,2,1,0:T(8,128)}, f32[3,8,64,128]{3,2,1,0:T(8,128)}) custom-call(f32[8]{0:T(128)} %eps_ref.1, f32[8]{0:T(128)} %sig_ref.1, s32[8]{0:T(128)} %wire_ref.1, f32[3,8,64,128]{3,2,1,0:T(8,128)} %e_hbm.1, f32[3,8,64,128]{3,2,1,0:T(8,128)} %h_hbm.1, s32[8,64,128]{2,1,0:T(8,128)} %mat_hbm.1, bf16[256,3840]{1,0:T(8,128)(2,1)} %constant.2.clone.strip_hbm), custom_call_target="tpu_custom_call" | custom-call | tf_op jit(solution)/shard_map/pallas_call | solution.py:650
  61.0 0.0 copy-start
  61.0 2.2 %copy.11 = f32[3,8,64,128]{3,2,1,0:T(8,128)} copy(f32[3,8,64,128]{3,2,1,0:T(8,128)} %get-tuple-element.4) | data formatting | bytes 1572864
  63.2 0.0 copy-done
  63.2 0.9 %copy.12 = f32[3,8,64,128]{3,2,1,0:T(8,128)} copy(f32[3,8,64,128]{3,2,1,0:T(8,128)S(1)} %copy-done) | data formatting | bytes 1572864
Async XLA Ops:
  61.0 2.2 %copy-start = (f32[3,8,64,128]{3,2,1,0:T(8,128)S(1)}, f32[3,8,64,128]{3,2,1,0:T(8,128)}, u32[]{:S(2)}) copy-start(f32[3,8,64,128]{3,2,1,0:T(8,128)} %get-tuple-element.5) | copy-start | bytes 2359300

commit v6 on v5

--- a/solution.py
+++ b/solution.py
@@ -511,11 +511,13 @@
             chosen = jnp.full((rows, cols), is_wire[z], jnp.int32) == 1
             for c in range(3):
                 dst[c, z] = jnp.where(chosen, filt[phase, c * n_wires + rank[z]], dst[c, z])
-
-    results = (
-        pltpu.make_async_copy(h_out, h_hbm_out, out_sem.at[0]),
-        pltpu.make_async_copy(e_out, e_hbm_out, out_sem.at[1]),
-    )
+            if phase == 1:
+                results[z].start()
+
+    results = [
+        pltpu.make_async_copy(e_out.at[:, z], e_hbm_out.at[:, z], out_sem.at[z]) for z in range(nz)
+    ]
+    results.append(pltpu.make_async_copy(h_out, h_hbm_out, out_sem.at[nz]))
 
     inputs[0].wait()
     pack_edges(0, e_ref, 0, 0)
@@ -591,7 +593,7 @@
     filter_edges()
     back(0)
     merge(0, h_out)
-    results[0].start()
+    results[nz].start()
     edges_back()
 
     kept = jnp.zeros((rows, cols), jnp.int32)
@@ -628,7 +630,6 @@
     filter_lines(1)
     back(1)
     merge(1, e_out)
-    results[1].start()
     drain(0)
     edges_gone()
     drain(1)
@@ -682,7 +683,7 @@
             dma((2, n_planes)),
             dma,
             dma((3,)),
-            dma((2,)),
+            dma((nz + 1,)),
             dma((4,)),
             dma((n_gy,)),
             dma((n_gy // 4,)),

time: 65 us -> 65 us (level)
  no operation moved by 1% of the time
where the time goes in v6:
time: 65 us; the launch traced here: 64.1 us
  Pallas kernels  60.4 us (93%)
  local copies, waits for them, and re-layouts  3.04 us (5%)
  between operations  0.65 us (1%)
    pallas_call x1, Pallas kernels, body(): pl.pallas_call(functools.partial(kernel, n_gx, n_gy, n_wires), out_shape=...  60.4 us
    unnamed x4, local copies, waits for them, and re-layouts  3.04 us

profile of v6, /device:TPU:1, one launch (start us, length us, event | category | flops | bytes accessed | tf_op | source)
XLA Modules:
  0.0 64.1 jit_solution(13361546917747662840)
XLA Ops:
  0.6 60.4 %shard_map.86 = (f32[3,8,64,128]{3,2,1,0:T(8,128)}, f32[3,8,64,128]{3,2,1,0:T(8,128)}) custom-call(f32[8]{0:T(128)} %eps_ref.1, f32[8]{0:T(128)} %sig_ref.1, s32[8]{0:T(128)} %wire_ref.1, f32[3,8,64,128]{3,2,1,0:T(8,128)} %e_hbm.1, f32[3,8,64,128]{3,2,1,0:T(8,128)} %h_hbm.1, s32[8,64,128]{2,1,0:T(8,128)} %mat_hbm.1, bf16[256,3840]{1,0:T(8,128)(2,1)} %constant.2.clone.strip_hbm), custom_call_target="tpu_custom_call" | custom-call | tf_op jit(solution)/shard_map/pallas_call | solution.py:651
  61.0 0.0 copy-start
  61.0 2.2 %copy.11 = f32[3,8,64,128]{3,2,1,0:T(8,128)} copy(f32[3,8,64,128]{3,2,1,0:T(8,128)} %get-tuple-element.4) | data formatting | bytes 1572864
  63.2 0.0 copy-done
  63.2 0.9 %copy.12 = f32[3,8,64,128]{3,2,1,0:T(8,128)} copy(f32[3,8,64,128]{3,2,1,0:T(8,128)S(1)} %copy-done) | data formatting | bytes 1572864
Async XLA Ops:
  61.0 2.2 %copy-start = (f32[3,8,64,128]{3,2,1,0:T(8,128)S(1)}, f32[3,8,64,128]{3,2,1,0:T(8,128)}, u32[]{:S(2)}) copy-start(f32[3,8,64,128]{3,2,1,0:T(8,128)} %get-tuple-element.5) | copy-start | bytes 2359300
